TPU v7x, 256 devices: a whole 4x4x8 slice. The times are simulated.
256 devices in a mesh: seq: 32 (over y, z_lo, core), head: 8 (over x, z_hi).
Axes of the slice: x: 4, y: 4, z: 8 (z_hi: 2, z_lo: 4; z = z_hi * 4 + z_lo), core: 2. Of those that a mesh axis runs over, the one named last changes fastest.
Arguments:
- tokens: bfloat16 [131072, 1024], P(('seq', 'head')), may hold values from -32 to 32
- w_qkv: bfloat16 [1024, 3072], P('seq'), may hold values from -0.1875 to 0.1875
- w_out: bfloat16 [1024, 1024], P('seq'), may hold values from -0.1875 to 0.1875
- neighbours: int32 [1024, 12], P('seq'), may hold values from 0 to 1023, as said below
Outputs:
- update: bfloat16 [131072, 1024], P(('seq', 'head'))
Inputs may be any that keep to these rules, and one draw needn't show every extreme that they name: Block b has grid coordinates z = b // 16, y = (b // 4) % 4, x = b % 4. Each row lists b itself first, then 11 different blocks among its 26 neighbours at offsets -1, 0, 1 in each coordinate (z taken modulo 1024 // 16, y and x modulo 4).
All inputs are finite; a program needn't handle non-finite values.
Results may differ from a plain program's by a relative error of at most 0.0065.
The roundings to bfloat16 on the way count: a program that leaves them out, or rounds other values in their place, can miss the bound.
Values may be sent and summed in bfloat16 or wider, within the bound.
A program may use at most 64 MiB of HBM per device.

v0:
```python
import math
import jax
import jax.numpy as jnp
from jax import lax
from jax.sharding import PartitionSpec as P

HEADS = 8
HD = 128
BLK = 128
NBR = 12
PB = 16


def padded_2(cells, sides, width):
    for axis, dim in sides:
        count = lax.axis_size(axis)
        head = lax.slice_in_dim(cells, 0, width, axis=dim)
        tail = lax.slice_in_dim(cells, cells.shape[dim] - width, cells.shape[dim], axis=dim)
        cells = jnp.concatenate(
            [
                lax.ppermute(tail, axis, [(i, (i + 1) % count) for i in range(count)]),
                cells,
                lax.ppermute(head, axis, [((i + 1) % count, i) for i in range(count)]),
            ],
            axis=dim,
        )
    return cells


def local(tokens, w_qkv, w_out, neighbours):
    head_count = lax.axis_size("head")
    seq_count = lax.axis_size("seq")
    per_device = HEADS // head_count
    local_rows = tokens.shape[0]
    slab_rows = local_rows * head_count
    full_qkv = lax.all_gather(w_qkv, "seq", axis=0, tiled=True)
    projected = jnp.dot(tokens, full_qkv, preferred_element_type=jnp.float32)
    projected = projected.astype(jnp.bfloat16).reshape(local_rows, 3, HEADS, HD)
    slab = lax.all_to_all(projected, "head", split_axis=2, concat_axis=0, tiled=True)
    queries = slab[:, 0]
    key_value = slab[:, 1:3]
    padded = padded_2(key_value, (("seq", 0),), PB * BLK)
    kv_blocks = padded.reshape(-1, BLK, 2, per_device, HD)
    block_count = neighbours.shape[0]
    first_block = lax.axis_index("seq") * block_count
    local_lists = jnp.mod(neighbours - first_block + PB, block_count * seq_count)
    group_blocks = 4
    scale = 1.0 / math.sqrt(HD)

    def attend(args):
        query_group, list_group = args
        picked = kv_blocks[list_group].reshape(group_blocks, NBR * BLK, 2, per_device, HD)
        keys = picked[:, :, 0]
        values = picked[:, :, 1]
        scores = (
            jnp.einsum("nqhd,nkhd->nhqk", query_group, keys, preferred_element_type=jnp.float32)
            * scale
        )
        largest = jnp.max(scores, axis=-1, keepdims=True)
        expo = jnp.exp(scores - largest)
        probs = (expo / jnp.sum(expo, axis=-1, keepdims=True)).astype(jnp.bfloat16)
        result = jnp.einsum("nhqk,nkhd->nqhd", probs, values, preferred_element_type=jnp.float32)
        return result.astype(jnp.bfloat16)

    grouped_q = queries.reshape(block_count // group_blocks, group_blocks, BLK, per_device, HD)
    grouped_l = local_lists.reshape(block_count // group_blocks, group_blocks, NBR)
    attended = lax.map(attend, (grouped_q, grouped_l)).reshape(slab_rows, per_device, HD)
    returned = lax.all_to_all(attended, "head", split_axis=0, concat_axis=1, tiled=True)
    flat = returned.reshape(local_rows, HEADS * HD)
    full_out = lax.all_gather(w_out, "seq", axis=0, tiled=True)
    update = jnp.dot(flat, full_out, preferred_element_type=jnp.float32)
    return update.astype(jnp.bfloat16)


def solution(mesh):
    return jax.shard_map(
        local,
        mesh=mesh,
        in_specs=(P(("seq", "head"), None), P("seq", None), P("seq", None), P("seq", None)),
        out_specs=P(("seq", "head"), None),
        check_vma=False,
    )
```

profile of v0, /device:TPU:33, one launch (start us, length us, event | category | flops | bytes accessed | tf_op | source)
XLA Modules:
  0.0 384.4 jit_solution(7192390426923187747)
XLA Ops:
  7.3 71.2 %all-gather.3.cloned.1.call-done = bf16[1024,3072]{1,0:T(8,128)(2,1)} async-done(((bf16[32,3072]{1,0:T(8,128)(2,1)}), bf16[1024,3072]{1,0:T(8,128)(2,1)}) %all-gather.3.cloned.1.call-update) | async-done | bytes 6291472 | tf_op jit(solution)/shard_map/all_gather | solution.py:36
  78.5 6.4 %fusion.29 = bf16[64,8,24,128]{3,1,2,0:T(8,128)(2,1)S(1)} fusion(bf16[512,1024]{1,0:T(8,128)(2,1)S(1)} %copy-done, bf16[1024,3072]{1,0:T(8,128)(2,1)} %all-gather.3.cloned.1.call-done), kind=kOutput, calls=%fused_computation.27 | convolution fusion | flops 3222798336 | bytes 10485760 | tf_op jit(solution)/shard_map/dot_general | solution.py:37
  86.5 82.3 %all_to_all.33 = bf16[512,3,8,128]{3,0,1,2:T(8,128)(2,1)S(1)} all-to-all(bf16[512,3,8,128]{3,0,1,2:T(8,128)(2,1)S(1)} %copy.20), channel_id=1, replica_groups=mesh['seq'=32,'head'=8] {'head'}, dimensions={2} | all-to-all | bytes 6291456 | tf_op jit(solution)/shard_map/all_to_all | solution.py:39
  169.1 1.6 copy-done.1
  171.9 2.4 collective-permute-start
  174.4 1.7 slice.29
  176.2 2.3 slice.31
  178.5 16.8 %collective-permute-done = bf16[2048,2,1,128]{3,0,1,2:T(8,128)(2,1)} collective-permute-done((bf16[2048,2,1,128]{3,0,1,2:T(8,128)(2,1)}, bf16[2048,2,1,128]{3,0,1,2:T(8,128)(2,1)}, u32[]{:S(2)}, u32[]{:S(2)}) %collective-permute-start) | collective-permute-done | bytes 1048608 | tf_op jit(solution)/shard_map/ppermute | solution.py:21
  195.2 8.9 %collective-permute-done.1 = bf16[2048,2,1,128]{3,0,1,2:T(8,128)(2,1)} collective-permute-done((bf16[2048,2,1,128]{3,0,1,2:T(8,128)(2,1)S(1)}, bf16[2048,2,1,128]{3,0,1,2:T(8,128)(2,1)}, u32[]{:S(2)}, u32[]{:S(2)}) %collective-permute-start.1) | collective-permute-done | bytes 1048608 | tf_op jit(solution)/shard_map/ppermute | solution.py:23
  204.2 1.7 pad_maximum_fusion
  205.9 2.2 copy.22
  208.1 123.6 %while.10 = (s32[]{:T(128)}, bf16[8,4,128,1,128]{4,2,1,0,3:T(8,128)(2,1)S(1)}, s32[8,4,12]{2,1,0:T(4,128)S(1)}, bf16[64,128,2,1,128]{4,1,3,2,0:T(8,128)(2,1)}, bf16[8,4,128,1,128]{4,2,1,3,0:T(8,128)(2,1)}, /*index=5*/s32[]{:T(128)}) while((s32[]{:T(128)}, bf16[8,4,128,1,128]{4,2,1,0,3:T(8,128)(2,1)S(1)}, s32[8,4,12]{2,1,0:T(4,128)S(1)}, ...), condition=%wide.region_3.4_spmd, body=%wide.region_0.3_spmd.sunk | while | flops 609555072 | bytes 18229452 | solution.py:67
  208.2 4.9 %gather_fusion = bf16[48,128,2,128]{3,1,2,0:T(8,128)(2,1)} fusion(bf16[64,128,2,128]{3,1,2,0:T(8,128)(2,1)} %bitcast.87, s32[1024]{0:T(1024)S(1)} %pad_clamp_fusion.2), kind=kCustom, calls=%fused_computation.clone.1 | custom fusion | bytes 6291648 | tf_op jit(solution)/shard_map/while/body/eval_jaxpr/gather | solution.py:52
  213.2 4.0 %copy.35 = bf16[48,128,2,128]{3,1,0,2:T(8,128)(2,1)} copy(bf16[48,128,2,128]{3,1,2,0:T(8,128)(2,1)} %gather_fusion) | data formatting | bytes 6291456 | tf_op jit(solution)/shard_map/while/body/eval_jaxpr/gather | solution.py:52
  217.2 2.6 fusion.45
  219.8 3.7 fusion.46
  223.7 4.9 %gather_fusion = bf16[48,128,2,128]{3,1,2,0:T(8,128)(2,1)} fusion(bf16[64,128,2,128]{3,1,2,0:T(8,128)(2,1)} %bitcast.87, s32[1024]{0:T(1024)S(1)} %pad_clamp_fusion.2), kind=kCustom, calls=%fused_computation.clone.1 | custom fusion | bytes 6291648 | tf_op jit(solution)/shard_map/while/body/eval_jaxpr/gather | solution.py:52
  228.7 4.0 %copy.35 = bf16[48,128,2,128]{3,1,0,2:T(8,128)(2,1)} copy(bf16[48,128,2,128]{3,1,2,0:T(8,128)(2,1)} %gather_fusion) | data formatting | bytes 6291456 | tf_op jit(solution)/shard_map/while/body/eval_jaxpr/gather | solution.py:52
  232.7 2.6 fusion.45
  235.2 3.6 fusion.46
  239.2 4.9 %gather_fusion = bf16[48,128,2,128]{3,1,2,0:T(8,128)(2,1)} fusion(bf16[64,128,2,128]{3,1,2,0:T(8,128)(2,1)} %bitcast.87, s32[1024]{0:T(1024)S(1)} %pad_clamp_fusion.2), kind=kCustom, calls=%fused_computation.clone.1 | custom fusion | bytes 6291648 | tf_op jit(solution)/shard_map/while/body/eval_jaxpr/gather | solution.py:52
  244.1 4.0 %copy.35 = bf16[48,128,2,128]{3,1,0,2:T(8,128)(2,1)} copy(bf16[48,128,2,128]{3,1,2,0:T(8,128)(2,1)} %gather_fusion) | data formatting | bytes 6291456 | tf_op jit(solution)/shard_map/while/body/eval_jaxpr/gather | solution.py:52
  248.1 2.6 fusion.45
  250.7 3.6 fusion.46
  254.6 4.9 %gather_fusion = bf16[48,128,2,128]{3,1,2,0:T(8,128)(2,1)} fusion(bf16[64,128,2,128]{3,1,2,0:T(8,128)(2,1)} %bitcast.87, s32[1024]{0:T(1024)S(1)} %pad_clamp_fusion.2), kind=kCustom, calls=%fused_computation.clone.1 | custom fusion | bytes 6291648 | tf_op jit(solution)/shard_map/while/body/eval_jaxpr/gather | solution.py:52
  259.5 4.0 %copy.35 = bf16[48,128,2,128]{3,1,0,2:T(8,128)(2,1)} copy(bf16[48,128,2,128]{3,1,2,0:T(8,128)(2,1)} %gather_fusion) | data formatting | bytes 6291456 | tf_op jit(solution)/shard_map/while/body/eval_jaxpr/gather | solution.py:52
  263.6 2.6 fusion.45
  266.1 3.6 fusion.46
  270.1 4.9 %gather_fusion = bf16[48,128,2,128]{3,1,2,0:T(8,128)(2,1)} fusion(bf16[64,128,2,128]{3,1,2,0:T(8,128)(2,1)} %bitcast.87, s32[1024]{0:T(1024)S(1)} %pad_clamp_fusion.2), kind=kCustom, calls=%fused_computation.clone.1 | custom fusion | bytes 6291648 | tf_op jit(solution)/shard_map/while/body/eval_jaxpr/gather | solution.py:52
  275.0 4.0 %copy.35 = bf16[48,128,2,128]{3,1,0,2:T(8,128)(2,1)} copy(bf16[48,128,2,128]{3,1,2,0:T(8,128)(2,1)} %gather_fusion) | data formatting | bytes 6291456 | tf_op jit(solution)/shard_map/while/body/eval_jaxpr/gather | solution.py:52
  279.0 2.6 fusion.45
  281.6 3.6 fusion.46
  285.5 4.9 %gather_fusion = bf16[48,128,2,128]{3,1,2,0:T(8,128)(2,1)} fusion(bf16[64,128,2,128]{3,1,2,0:T(8,128)(2,1)} %bitcast.87, s32[1024]{0:T(1024)S(1)} %pad_clamp_fusion.2), kind=kCustom, calls=%fused_computation.clone.1 | custom fusion | bytes 6291648 | tf_op jit(solution)/shard_map/while/body/eval_jaxpr/gather | solution.py:52
  290.4 4.0 %copy.35 = bf16[48,128,2,128]{3,1,0,2:T(8,128)(2,1)} copy(bf16[48,128,2,128]{3,1,2,0:T(8,128)(2,1)} %gather_fusion) | data formatting | bytes 6291456 | tf_op jit(solution)/shard_map/while/body/eval_jaxpr/gather | solution.py:52
  294.4 2.6 fusion.45
  297.0 3.6 fusion.46
  300.9 4.9 %gather_fusion = bf16[48,128,2,128]{3,1,2,0:T(8,128)(2,1)} fusion(bf16[64,128,2,128]{3,1,2,0:T(8,128)(2,1)} %bitcast.87, s32[1024]{0:T(1024)S(1)} %pad_clamp_fusion.2), kind=kCustom, calls=%fused_computation.clone.1 | custom fusion | bytes 6291648 | tf_op jit(solution)/shard_map/while/body/eval_jaxpr/gather | solution.py:52
  305.9 4.0 %copy.35 = bf16[48,128,2,128]{3,1,0,2:T(8,128)(2,1)} copy(bf16[48,128,2,128]{3,1,2,0:T(8,128)(2,1)} %gather_fusion) | data formatting | bytes 6291456 | tf_op jit(solution)/shard_map/while/body/eval_jaxpr/gather | solution.py:52
  309.9 2.6 fusion.45
  312.5 3.6 fusion.46
  316.4 4.9 %gather_fusion = bf16[48,128,2,128]{3,1,2,0:T(8,128)(2,1)} fusion(bf16[64,128,2,128]{3,1,2,0:T(8,128)(2,1)} %bitcast.87, s32[1024]{0:T(1024)S(1)} %pad_clamp_fusion.2), kind=kCustom, calls=%fused_computation.clone.1 | custom fusion | bytes 6291648 | tf_op jit(solution)/shard_map/while/body/eval_jaxpr/gather | solution.py:52
  321.3 4.0 %copy.35 = bf16[48,128,2,128]{3,1,0,2:T(8,128)(2,1)} copy(bf16[48,128,2,128]{3,1,2,0:T(8,128)(2,1)} %gather_fusion) | data formatting | bytes 6291456 | tf_op jit(solution)/shard_map/while/body/eval_jaxpr/gather | solution.py:52
  325.3 2.6 fusion.45
  327.9 3.6 fusion.46
  334.0 32.8 %all_to_all.34 = bf16[8,2,32768]{2,1,0:T(2,128)(2,1)} all-to-all(bf16[8,2,32768]{2,1,0:T(2,128)(2,1)S(1)} %reshape.97), channel_id=1, replica_groups=mesh['seq'=32,'head'=8] {'head'}, dimensions={0} | all-to-all | bytes 2097152 | tf_op jit(solution)/shard_map/all_to_all | solution.py:68
  366.8 4.3 %reshape.98 = bf16[4096,1,128]{2,1,0:T(2,128)(2,1)S(1)} reshape(bf16[8,2,32768]{2,1,0:T(2,128)(2,1)} %all_to_all.34) | data formatting | bytes 2097152
  372.2 1.5 copy.26
  373.7 3.8 convolution_convert_fusion.1
  (62 shorter events, 9.2 us)
Async XLA Ops:
  6.5 71.9 %copy-start = (bf16[512,1024]{1,0:T(8,128)(2,1)S(1)}, bf16[512,1024]{1,0:T(8,128)(2,1)}, u32[]{:S(2)}) copy-start(bf16[512,1024]{1,0:T(8,128)(2,1)} %param.6) | copy-start | bytes 3145732
  6.5 71.9 %all-gather.3.cloned.1.call-start = ((), (), s32[]{:S(2)}) async-start(), calls=%async_computation.2 | async-start | bytes 6488064 | tf_op jit(solution)/shard_map/all_gather | solution.py:36
  7.3 366.5 %all-gather.5.cloned.1.call-start = ((), (), s32[]{:S(2)}) async-start(), calls=%async_computation.3 | async-start | bytes 2162688 | tf_op jit(solution)/shard_map/all_gather | solution.py:70
  169.1 1.7 copy-start.1
  169.1 5.2 %copy-start.2 = (s32[32,12]{0,1:T(8,128)S(1)}, s32[32,12]{0,1:T(8,128)}, u32[]{:S(2)}) copy-start(s32[32,12]{0,1:T(8,128)} %param.9) | copy-start | bytes 4612
  171.9 23.4 %collective-permute-start = (bf16[2048,2,1,128]{3,0,1,2:T(8,128)(2,1)}, bf16[2048,2,1,128]{3,0,1,2:T(8,128)(2,1)}, u32[]{:S(2)}, u32[]{:S(2)}) collective-permute-start(bf16[2048,2,1,128]{3,0,1,2:T(8,128)(2,1)} %get-tuple-element.53), channel_id=1, source_target_pairs={{0,8},{8,16},{16,24},{24,32},{32,40},{40,48},{48,56},{56,64},{64,7... | collective-permute-start | bytes 3145736 | tf_op jit(solution)/shard_map/ppermute | solution.py:21
  174.3 29.9 %collective-permute-start.1 = (bf16[2048,2,1,128]{3,0,1,2:T(8,128)(2,1)S(1)}, bf16[2048,2,1,128]{3,0,1,2:T(8,128)(2,1)}, u32[]{:S(2)}, u32[]{:S(2)}) collective-permute-start(bf16[2048,2,1,128]{3,0,1,2:T(8,128)(2,1)S(1)} %get-tuple-element.54), channel_id=1, source_target_pairs={{8,0},{16,8},{24,16},{32,24},{40,32},{48,40},{56,48},{64,56},{72,6... | collective-permute-start | bytes 3145736 | tf_op jit(solution)/shard_map/ppermute | solution.py:23
Sparse Core Ops, SparseCore 0:
  9.2 69.2 all-gather.2
  174.4 60.0 all-gather.4
where the time goes:
time: 386 us; the launch traced here: 384 us
  blocking collectives  115 us (30%)
  waiting for transfers between devices  97.6 us (25%)
  local copies, waits for them, and re-layouts  92.1 us (24%)
  matrix products  59.9 us (16%)
  between operations  13.5 us (3%)
    all_to_all x1, blocking collectives, local(): lax.all_to_all(projected, 'head', split_axis=2, concat_axis=0, tiled=True)  82.3 us
    gather x16, local copies, waits for them, and re-layouts, attend(): kv_blocks[list_group].reshape(group_blocks, NBR * BLK, 2, per_device, HD)  71.6 us
    all_gather x1, waiting for transfers between devices, local(): full_qkv = lax.all_gather(w_qkv, 'seq', axis=0, tiled=True)  71.2 us
    all_to_all x1, blocking collectives, local(): lax.all_to_all(attended, 'head', split_axis=0, concat_axis=1, tiled=True)  32.8 us
    dot_general x8, matrix products, attend(): jnp.einsum('nhqk,nkhd->nqhd', probs, values, preferred_element_type=jnp.f...  29.2 us
    sub x8, matrix products, attend(): expo = jnp.exp(scores - largest)  20.5 us
    ppermute x1, waiting for transfers between devices, padded_2(): lax.ppermute(tail, axis, [(i, (i + 1) % count) for i in range(count)])  16.8 us
    ppermute x1, waiting for transfers between devices, padded_2(): lax.ppermute(head, axis, [((i + 1) % count, i) for i in range(count)])  8.94 us
  transfers between devices with their start and end apart: 4, of which 3 were waited for; matrix products, arithmetic and copies ran while one was open for 37% of the time, Pallas kernels for 0%

commit v1 on v0

--- a/solution.py
+++ b/solution.py
@@ -33,7 +33,16 @@
     per_device = HEADS // head_count
     local_rows = tokens.shape[0]
     slab_rows = local_rows * head_count
-    full_qkv = lax.all_gather(w_qkv, "seq", axis=0, tiled=True)
+    detail_goods_here = lambda patch: jnp.concatenate(
+        jax.lax.all_to_all(
+            jnp.stack([patch] * jax.lax.axis_size("seq"), 0),
+            axis_name="seq",
+            split_axis=0,
+            concat_axis=0,
+        ),
+        0,
+    )
+    full_qkv = detail_goods_here(w_qkv)
     projected = jnp.dot(tokens, full_qkv, preferred_element_type=jnp.float32)
     projected = projected.astype(jnp.bfloat16).reshape(local_rows, 3, HEADS, HD)
     slab = lax.all_to_all(projected, "head", split_axis=2, concat_axis=0, tiled=True)

time: 386 us -> 453 us (1.17)
  the two profiles are of different devices: /device:TPU:33 before, /device:TPU:48 now
where the time goes in v1:
time: 453 us; the launch traced here: 451 us
  blocking collectives  264 us (58%)
  local copies, waits for them, and re-layouts  94 us (21%)
  matrix products  57.1 us (13%)
  waiting for transfers between devices  17.7 us (4%)
  between operations  13.5 us (3%)
    all_to_all x1, blocking collectives, local(): jax.lax.all_to_all(jnp.stack([patch] * jax.lax.axis_size('seq'), 0), axis...  145 us
    all_to_all x1, blocking collectives, local(): lax.all_to_all(projected, 'head', split_axis=2, concat_axis=0, tiled=True)  83.6 us
    gather x16, local copies, waits for them, and re-layouts, attend(): kv_blocks[list_group].reshape(group_blocks, NBR * BLK, 2, per_device, HD)  71.6 us
    all_to_all x1, blocking collectives, local(): lax.all_to_all(attended, 'head', split_axis=0, concat_axis=1, tiled=True)  34.7 us
    dot_general x8, matrix products, attend(): jnp.einsum('nhqk,nkhd->nqhd', probs, values, preferred_element_type=jnp.f...  29.1 us
    sub x8, matrix products, attend(): expo = jnp.exp(scores - largest)  20.5 us
    ppermute x1, waiting for transfers between devices, padded_2(): lax.ppermute(tail, axis, [(i, (i + 1) % count) for i in range(count)])  15.8 us
  transfers between devices with their start and end apart: 3, of which 2 were waited for; matrix products, arithmetic and copies ran while one was open for 31% of the time, Pallas kernels for 0%

profile of v1, /device:TPU:48, one launch (start us, length us, event | category | flops | bytes accessed | tf_op | source)
XLA Modules:
  0.0 451.2 jit_solution(6694071674010428455)
XLA Ops:
  6.5 1.8 stack.2
  8.3 145.2 %all_to_all.38 = bf16[32,32,3072]{2,1,0:T(8,128)(2,1)S(1)} all-to-all(bf16[32,32,3072]{2,1,0:T(8,128)(2,1)S(1)} %stack.2), channel_id=1, replica_groups=mesh['seq'=32,'head'=8] {'seq'}, dimensions={0} | all-to-all | bytes 12582912 | tf_op jit(solution)/shard_map/all_to_all | solution.py:37
  153.6 3.7 fusion.29
  158.8 83.6 %all_to_all.39 = bf16[512,3,8,128]{3,0,1,2:T(8,128)(2,1)S(1)} all-to-all(bf16[512,3,8,128]{3,0,1,2:T(8,128)(2,1)S(1)} %copy.20), channel_id=1, replica_groups=mesh['seq'=32,'head'=8] {'head'}, dimensions={2} | all-to-all | bytes 6291456 | tf_op jit(solution)/shard_map/all_to_all | solution.py:48
  242.7 1.6 copy-done.1
  245.5 1.7 collective-permute-start.1
  247.4 1.7 slice.29
  249.1 2.3 slice.31
  251.5 15.8 %collective-permute-done = bf16[2048,2,1,128]{3,0,1,2:T(8,128)(2,1)} collective-permute-done((bf16[2048,2,1,128]{3,0,1,2:T(8,128)(2,1)}, bf16[2048,2,1,128]{3,0,1,2:T(8,128)(2,1)}, u32[]{:S(2)}, u32[]{:S(2)}) %collective-permute-start) | collective-permute-done | bytes 1048608 | tf_op jit(solution)/shard_map/ppermute | solution.py:21
  267.3 1.8 collective-permute-done.1
  269.1 1.7 pad_maximum_fusion
  270.8 2.2 copy.22
  273.0 123.6 %while.10 = (s32[]{:T(128)}, bf16[8,4,128,1,128]{4,2,1,0,3:T(8,128)(2,1)S(1)}, s32[8,4,12]{2,1,0:T(4,128)S(1)}, bf16[64,128,2,1,128]{4,1,3,2,0:T(8,128)(2,1)}, bf16[8,4,128,1,128]{4,2,1,3,0:T(8,128)(2,1)}, /*index=5*/s32[]{:T(128)}) while((s32[]{:T(128)}, bf16[8,4,128,1,128]{4,2,1,0,3:T(8,128)(2,1)S(1)}, s32[8,4,12]{2,1,0:T(4,128)S(1)}, ...), condition=%wide.region_3.4_spmd, body=%wide.region_0.3_spmd.sunk | while | flops 609555072 | bytes 18229452 | solution.py:76
  273.1 4.9 %gather_fusion = bf16[48,128,2,128]{3,1,2,0:T(8,128)(2,1)} fusion(bf16[64,128,2,128]{3,1,2,0:T(8,128)(2,1)} %bitcast.88, s32[1024]{0:T(1024)S(1)} %pad_clamp_fusion.2), kind=kCustom, calls=%fused_computation.clone.1 | custom fusion | bytes 6291648 | tf_op jit(solution)/shard_map/while/body/eval_jaxpr/gather | solution.py:61
  278.1 4.0 copy.35
  282.1 2.6 fusion.45
  284.7 3.7 fusion.46
  288.6 5.0 %gather_fusion = bf16[48,128,2,128]{3,1,2,0:T(8,128)(2,1)} fusion(bf16[64,128,2,128]{3,1,2,0:T(8,128)(2,1)} %bitcast.88, s32[1024]{0:T(1024)S(1)} %pad_clamp_fusion.2), kind=kCustom, calls=%fused_computation.clone.1 | custom fusion | bytes 6291648 | tf_op jit(solution)/shard_map/while/body/eval_jaxpr/gather | solution.py:61
  293.6 4.0 copy.35
  297.6 2.6 fusion.45
  300.2 3.6 fusion.46
  304.1 4.9 %gather_fusion = bf16[48,128,2,128]{3,1,2,0:T(8,128)(2,1)} fusion(bf16[64,128,2,128]{3,1,2,0:T(8,128)(2,1)} %bitcast.88, s32[1024]{0:T(1024)S(1)} %pad_clamp_fusion.2), kind=kCustom, calls=%fused_computation.clone.1 | custom fusion | bytes 6291648 | tf_op jit(solution)/shard_map/while/body/eval_jaxpr/gather | solution.py:61
  309.0 4.0 copy.35
  313.1 2.6 fusion.45
  315.6 3.6 fusion.46
  319.6 4.9 %gather_fusion = bf16[48,128,2,128]{3,1,2,0:T(8,128)(2,1)} fusion(bf16[64,128,2,128]{3,1,2,0:T(8,128)(2,1)} %bitcast.88, s32[1024]{0:T(1024)S(1)} %pad_clamp_fusion.2), kind=kCustom, calls=%fused_computation.clone.1 | custom fusion | bytes 6291648 | tf_op jit(solution)/shard_map/while/body/eval_jaxpr/gather | solution.py:61
  324.5 4.0 copy.35
  328.5 2.6 fusion.45
  331.1 3.6 fusion.46
  335.0 4.9 %gather_fusion = bf16[48,128,2,128]{3,1,2,0:T(8,128)(2,1)} fusion(bf16[64,128,2,128]{3,1,2,0:T(8,128)(2,1)} %bitcast.88, s32[1024]{0:T(1024)S(1)} %pad_clamp_fusion.2), kind=kCustom, calls=%fused_computation.clone.1 | custom fusion | bytes 6291648 | tf_op jit(solution)/shard_map/while/body/eval_jaxpr/gather | solution.py:61
  339.9 4.0 copy.35
  344.0 2.6 fusion.45
  346.5 3.6 fusion.46
  350.5 4.9 %gather_fusion = bf16[48,128,2,128]{3,1,2,0:T(8,128)(2,1)} fusion(bf16[64,128,2,128]{3,1,2,0:T(8,128)(2,1)} %bitcast.88, s32[1024]{0:T(1024)S(1)} %pad_clamp_fusion.2), kind=kCustom, calls=%fused_computation.clone.1 | custom fusion | bytes 6291648 | tf_op jit(solution)/shard_map/while/body/eval_jaxpr/gather | solution.py:61
  355.4 4.0 copy.35
  359.4 2.6 fusion.45
  362.0 3.6 fusion.46
  365.9 4.9 %gather_fusion = bf16[48,128,2,128]{3,1,2,0:T(8,128)(2,1)} fusion(bf16[64,128,2,128]{3,1,2,0:T(8,128)(2,1)} %bitcast.88, s32[1024]{0:T(1024)S(1)} %pad_clamp_fusion.2), kind=kCustom, calls=%fused_computation.clone.1 | custom fusion | bytes 6291648 | tf_op jit(solution)/shard_map/while/body/eval_jaxpr/gather | solution.py:61
  370.8 4.0 copy.35
  374.9 2.6 fusion.45
  377.4 3.6 fusion.46
  381.4 4.9 %gather_fusion = bf16[48,128,2,128]{3,1,2,0:T(8,128)(2,1)} fusion(bf16[64,128,2,128]{3,1,2,0:T(8,128)(2,1)} %bitcast.88, s32[1024]{0:T(1024)S(1)} %pad_clamp_fusion.2), kind=kCustom, calls=%fused_computation.clone.1 | custom fusion | bytes 6291648 | tf_op jit(solution)/shard_map/while/body/eval_jaxpr/gather | solution.py:61
  386.3 4.0 copy.35
  390.3 2.6 fusion.45
  392.9 3.6 fusion.46
  398.9 34.7 %all_to_all.40 = bf16[8,2,32768]{2,1,0:T(2,128)(2,1)} all-to-all(bf16[8,2,32768]{2,1,0:T(2,128)(2,1)S(1)} %reshape.103), channel_id=1, replica_groups=mesh['seq'=32,'head'=8] {'head'}, dimensions={0} | all-to-all | bytes 2097152 | tf_op jit(solution)/shard_map/all_to_all | solution.py:77
  433.6 4.3 reshape.104
  440.6 3.8 convolution_convert_fusion.1
  (61 shorter events, 9.9 us)
Async XLA Ops:
  6.5 147.0 %copy-start = (bf16[512,1024]{1,0:T(8,128)(2,1)S(1)}, bf16[512,1024]{1,0:T(8,128)(2,1)}, u32[]{:S(2)}) copy-start(bf16[512,1024]{1,0:T(8,128)(2,1)} %param.6) | copy-start | bytes 3145732
  6.5 434.0 %all-gather.2.cloned.1.call-start = ((), (), s32[]{:S(2)}) async-start(), calls=%async_computation.3 | async-start | bytes 2162688 | tf_op jit(solution)/shard_map/all_gather | solution.py:79
  242.7 1.7 copy-start.1
  242.7 4.6 %copy-start.2 = (s32[32,12]{0,1:T(8,128)S(1)}, s32[32,12]{0,1:T(8,128)}, u32[]{:S(2)}) copy-start(s32[32,12]{0,1:T(8,128)} %param.9) | copy-start | bytes 4612
  245.5 21.8 %collective-permute-start = (bf16[2048,2,1,128]{3,0,1,2:T(8,128)(2,1)}, bf16[2048,2,1,128]{3,0,1,2:T(8,128)(2,1)}, u32[]{:S(2)}, u32[]{:S(2)}) collective-permute-start(bf16[2048,2,1,128]{3,0,1,2:T(8,128)(2,1)} %get-tuple-element.53), channel_id=1, source_target_pairs={{0,8},{8,16},{16,24},{24,32},{32,40},{40,48},{48,56},{56,64},{64,7... | collective-permute-start | bytes 3145736 | tf_op jit(solution)/shard_map/ppermute | solution.py:21
  245.5 23.6 %collective-permute-start.1 = (bf16[2048,2,1,128]{3,0,1,2:T(8,128)(2,1)S(1)}, bf16[2048,2,1,128]{3,0,1,2:T(8,128)(2,1)}, u32[]{:S(2)}, u32[]{:S(2)}) collective-permute-start(bf16[2048,2,1,128]{3,0,1,2:T(8,128)(2,1)S(1)} %get-tuple-element.54), channel_id=1, source_target_pairs={{8,0},{16,8},{24,16},{32,24},{40,32},{48,40},{56,48},{64,56},{72,6... | collective-permute-start | bytes 3145736 | tf_op jit(solution)/shard_map/ppermute | solution.py:23
Sparse Core Ops, SparseCore 0:
  247.4 62.1 all-gather.1
